TPU v7x, 32 devices: a whole 2x2x4 slice. The times are simulated.
32 devices in a mesh: groups: 2 (over x), row: 16 (over z, y, core).
Axes of the slice: x: 2, y: 2, z: 4, core: 2. Of those that a mesh axis runs over, the one named last changes fastest.
Arguments:
- walkers: bfloat16 [512, 256, 64], P(('groups', 'row')), parts along dimension 0, may hold values from -6 to 6
- inv_intersection: bfloat16 [512, 64, 64], P(('groups', 'row')), parts along dimension 0, may hold values from -0.75 to 0.75
- copies: int32 [512], P(('groups', 'row')), parts along dimension 0, may hold values from 0 to 3, as said below
- deal: int32 [32], P('groups'), parts along dimension 0, may hold values from 0 to 15, each once
- trial: bfloat16 [512, 64], P('groups'), parts along dimension 0, may hold values from -6 to 6
- chol: bfloat16 [8192, 256, 256], P('groups', 'row'), parts along dimension 0, may hold values from -0.15625 to 0.15625
- noise: float32 [512, 4096], P(('groups', 'row')), parts along dimension 0, may hold values from -6 to 6
Outputs:
- propagated: bfloat16 [512, 256, 64], P(('groups', 'row')), parts along dimension 0
- force_bias: float32 [512, 4096], P(('groups', 'row')), parts along dimension 0
There are 2 independent parts, one for each index of `groups`. A program takes and returns all parts, laid end to end along the dimension named above; each array names one. Nothing has to cross between parts.
Inputs may be any that keep to these rules, and one draw needn't show every extreme that they name: The copy counts sum to 256; the walkers of one device have at most 32 copies together, and some device reaches that.
All inputs are finite; a program needn't handle non-finite values.
Results may differ from a plain program's by a relative error of at most 0.023.
Values may be sent and summed in bfloat16 or wider, within the bound.
A program may use at most 128 MiB of HBM per device.

v0:
```python
import jax
import jax.numpy as jnp
from jax import lax
from jax.sharding import PartitionSpec as P

root_step = 0.1


def local(walkers, inv_intersection, copies, deal, trial, chol, noise):
    devices = lax.axis_size("row")
    own_index = lax.axis_index("row")
    per_device = walkers.shape[0]
    everyone = lax.all_gather(copies, "row", axis=0, tiled=True)
    copy_ends = jnp.cumsum(everyone)
    copy_starts = copy_ends - everyone
    residue = jnp.argsort(deal)
    slot_ids = jnp.arange(per_device, dtype=jnp.int32)
    wanted = slot_ids * devices + residue[own_index]
    parent = jnp.searchsorted(copy_ends, wanted, side="right")
    capacity = (2 * per_device + devices - 1) // devices
    own_first = copy_starts[own_index * per_device]
    own_count = jnp.sum(copies)
    own_ends = jnp.cumsum(copies)
    picks = jnp.arange(capacity, dtype=jnp.int32)[None, :]
    first_hit = own_first + jnp.mod(residue[:, None] - own_first, devices)
    positions = (first_hit + picks * devices).reshape(-1)
    usable = positions < own_first + own_count
    local_walker = jnp.searchsorted(own_ends, positions - own_first, side="right")
    local_walker = jnp.minimum(local_walker, per_device - 1)
    keep_mask = usable[:, None, None]
    send_orbital = jnp.where(keep_mask, walkers[local_walker], jnp.zeros((), walkers.dtype))
    send_inverse = jnp.where(
        keep_mask, inv_intersection[local_walker], jnp.zeros((), inv_intersection.dtype)
    )
    got_orbital, got_inverse = (
        lax.all_to_all(send_orbital, "row", split_axis=0, concat_axis=0, tiled=True),
        lax.all_to_all(send_inverse, "row", split_axis=0, concat_axis=0, tiled=True),
    )
    source = parent // per_device
    source_first = copy_starts[source * per_device]
    source_hit = source_first + jnp.mod(residue[own_index] - source_first, devices)
    received_index = source * capacity + (wanted - source_hit) // devices
    orbitals = got_orbital[received_index]
    inverse = got_inverse[received_index]
    half_rotated = jnp.einsum(
        "wmk,wkn->wmn", orbitals, inverse, preferred_element_type=jnp.float32
    ).astype(jnp.bfloat16)
    whole_density = jnp.einsum(
        "win,kn->wik", half_rotated, trial, preferred_element_type=jnp.float32
    ).astype(jnp.bfloat16)
    density = lax.all_to_all(whole_density, "row", split_axis=1, concat_axis=0, tiled=True)
    all_walkers = density.shape[0]
    own_rows = chol.shape[1]
    width = chol.shape[2]
    chol_flat = chol.reshape(chol.shape[0], own_rows * width)
    density_flat = density.reshape(all_walkers, own_rows * width)
    bias_raw = lax.psum_scatter(
        lax.dot_general(
            density_flat, chol_flat, (((1,), (1,)), ((), ())), preferred_element_type=jnp.float32
        ).astype(jnp.bfloat16),
        "row",
        scatter_dimension=0,
        tiled=True,
    ).astype(jnp.float32)
    force_bias = root_step * bias_raw
    fields = (noise + jnp.clip(force_bias, -1.0, 1.0)).astype(jnp.bfloat16)
    propagator_part = jnp.dot(
        lax.all_gather(fields, "row", axis=0, tiled=True),
        chol_flat,
        preferred_element_type=jnp.float32,
    ).astype(jnp.bfloat16)
    propagator_part = propagator_part.reshape(all_walkers, own_rows, width)
    propagator = lax.all_to_all(propagator_part, "row", split_axis=0, concat_axis=1, tiled=True)
    current = orbitals
    summed = orbitals.astype(jnp.float32)
    for degree in range(1, 5):
        product = jnp.einsum(
            "wik,wkn->win", propagator, current, preferred_element_type=jnp.float32
        )
        current = (root_step / degree * product).astype(jnp.bfloat16)
        summed = summed + current.astype(jnp.float32)
    return (summed.astype(jnp.bfloat16), force_bias)


def solution(mesh):
    in_specs = (
        P(("groups", "row"), None, None),
        P(("groups", "row"), None, None),
        P(("groups", "row")),
        P("groups"),
        P("groups", None),
        P("groups", "row", None),
        P(("groups", "row"), None),
    )
    out_specs = (P(("groups", "row"), None, None), P(("groups", "row"), None))
    return jax.shard_map(local, mesh=mesh, in_specs=in_specs, out_specs=out_specs, check_vma=False)
```

profile of v0, /device:TPU:0, one launch (start us, length us, event | category | flops | bytes accessed | tf_op | source)
XLA Modules:
  0.0 340.0 jit_solution(5975468247891966408)
XLA Ops:
  7.2 1.5 reduce_sum.9
  8.7 1.2 dynamic-slice
  10.6 0.9 dynamic-update-slice
  11.4 13.8 %all-reduce = s32[256]{0:T(256)S(1)} all-reduce(s32[256]{0:T(256)S(1)} %dynamic-update-slice), channel_id=1, replica_groups=mesh['groups'=2,'row'=16] {'row'}, use_global_device_ids=true, to_apply=%add | all-reduce | flops 256 | bytes 2048
  25.8 1.9 sort.17
  29.6 0.7 fusion.16
  30.5 0.7 copy.14
  31.4 7.9 %while.48 = (s32[]{:T(128)}, u32[32]{0:T(128)S(1)}, u32[32]{0:T(128)S(1)}, s32[16]{0:T(128)S(1)}, s32[2]{0:T(128)S(1)}, /*index=5*/s32[16]{0:T(128)S(1)}, s32[]{:T(128)}, s32[]{:T(128)}, s32[]{:T(128)}, s32[]{}) while((s32[]{:T(128)}, u32[32]{0:T(128)S(1)}, u32[32]{0:T(128)S(1)}, s32[16]{0:T(128)S(1)}, s32[2]{0:T(128)S(1)}, ...), condition=%wide.region_6.7_spmd.clone, body=%wide.region_5.6_spmd.clone.sunk | while | flops 1508 | bytes 6344 | solution.py:28
  31.4 0.7 gather_fusion
  32.1 0.7 add_subtract_fusion.2
  33.0 0.7 gather_fusion
  33.7 0.7 add_subtract_fusion.2
  34.6 0.7 gather_fusion
  35.3 0.7 add_subtract_fusion.2
  36.1 0.7 gather_fusion
  36.8 0.7 add_subtract_fusion.2
  37.7 0.7 gather_fusion
  38.4 0.7 add_subtract_fusion.2
  39.3 0.6 gather_fusion.5
  40.1 1.1 reshape.170
  41.2 3.5 %all-to-all-start.1 = ((bf16[16,2,4096]{2,1,0:T(2,128)(2,1)}), bf16[16,2,4096]{2,1,0:T(2,128)(2,1)S(1)}, u32[]{:S(2)}, u32[]{:S(2)}) async-start(bf16[16,2,4096]{2,1,0:T(2,128)(2,1)} %reshape.170), calls=%async_computation.1 | async-start | bytes 524288 | tf_op jit(solution)/shard_map/all_to_all | solution.py:37
  44.7 0.7 dynamic_slice.8
  46.0 1.1 broadcast_select_fusion.4
  47.2 7.5 %all-to-all-done.1 = bf16[16,2,4096]{2,1,0:T(2,128)(2,1)S(1)} async-done(((bf16[16,2,4096]{2,1,0:T(2,128)(2,1)}), bf16[16,2,4096]{2,1,0:T(2,128)(2,1)S(1)}, u32[]{:S(2)}, u32[]{:S(2)}) %all-to-all-start.1) | async-done | bytes 262176 | tf_op jit(solution)/shard_map/all_to_all | solution.py:37
  54.7 3.7 %all-to-all-start = ((bf16[32,256,64]{1,2,0:T(8,128)(2,1)}), bf16[32,256,64]{1,2,0:T(8,128)(2,1)S(1)}, u32[]{:S(2)}, u32[]{:S(2)}) async-start(bf16[32,256,64]{1,2,0:T(8,128)(2,1)} %broadcast_select_fusion.4), calls=%async_computation | async-start | bytes 2097152 | tf_op jit(solution)/shard_map/all_to_all | solution.py:36
  58.4 12.8 %while.49 = (s32[]{:T(128)}, u32[16]{0:T(128)S(1)}, u32[16]{0:T(128)S(1)}, s32[256]{0:T(256)S(1)}, s32[]{:T(128)}, /*index=5*/s32[]{:T(128)}, s32[]{:T(128)}, s32[]{}) while((s32[]{:T(128)}, u32[16]{0:T(128)S(1)}, u32[16]{0:T(128)S(1)}, s32[256]{0:T(256)S(1)}, s32[]{:T(128)}, /*index=5*/s32[]{:T(128)}, s32[]{:T(128)}, s32[]{}) %tuple.71), condition=%wide.region_8.9_spmd.clone, body=%wide.region_7.8_spmd.clone.sunk | while | flops 1268 | bytes 4976 | solution.py:19
  58.4 0.7 gather_fusion.1
  59.1 0.7 fusion.35
  59.8 0.7 gather_fusion.1
  60.5 0.7 fusion.35
  61.2 0.7 gather_fusion.1
  61.9 0.7 fusion.35
  62.7 0.7 gather_fusion.1
  63.3 0.7 fusion.35
  64.1 0.7 gather_fusion.1
  64.7 0.7 fusion.35
  65.5 0.7 gather_fusion.1
  66.2 0.7 fusion.35
  66.9 0.7 gather_fusion.1
  67.6 0.7 fusion.35
  68.3 0.7 gather_fusion.1
  69.0 0.7 fusion.35
  69.7 0.7 gather_fusion.1
  70.4 0.7 fusion.35
  71.2 0.7 gather_fusion.3
  71.8 0.7 compare_select_fusion.2
  73.5 7.7 %all-to-all-done = bf16[32,256,64]{1,2,0:T(8,128)(2,1)S(1)} async-done(((bf16[32,256,64]{1,2,0:T(8,128)(2,1)}), bf16[32,256,64]{1,2,0:T(8,128)(2,1)S(1)}, u32[]{:S(2)}, u32[]{:S(2)}) %all-to-all-start) | async-done | bytes 1048608 | tf_op jit(solution)/shard_map/all_to_all | solution.py:36
  81.8 1.0 convolution_convert_fusion.2
  82.8 2.5 copy.16
  85.3 6.7 %all-to-all-start.2 = ((bf16[16,256,256]{2,0,1:T(8,128)(2,1)}), bf16[16,256,256]{2,0,1:T(8,128)(2,1)S(1)}, u32[]{:S(2)}, u32[]{:S(2)}) async-start(bf16[16,256,256]{2,0,1:T(8,128)(2,1)} %copy.16), calls=%async_computation.2 | async-start | bytes 4194304 | tf_op jit(solution)/shard_map/all_to_all | solution.py:51
  92.1 22.6 %copy.21 = bf16[512,8,16,256]{3,1,2,0:T(8,128)(2,1)} copy(bf16[512,8,16,256]{3,2,1,0:T(8,128)(2,1)} %bitcast.42) | data formatting | bytes 67108864
  114.7 18.3 %all-to-all-done.2 = bf16[16,256,256]{2,0,1:T(8,128)(2,1)S(1)} async-done(((bf16[16,256,256]{2,0,1:T(8,128)(2,1)}), bf16[16,256,256]{2,0,1:T(8,128)(2,1)S(1)}, u32[]{:S(2)}, u32[]{:S(2)}) %all-to-all-start.2) | async-done | bytes 2097184 | tf_op jit(solution)/shard_map/all_to_all | solution.py:51
  133.0 0.9 copy.17
  133.9 1.0 copy.20
  134.9 15.7 %convolution_convert_fusion.1 = bf16[256,4096]{1,0:T(8,128)(2,1)} fusion(bf16[256,4096]{1,0:T(8,128)(2,1)S(1)} %bitcast.50, bf16[4096,4096]{1,0:T(8,128)(2,1)} %bitcast.43), kind=kOutput, calls=%fused_computation.24 | convolution fusion | flops 8590983168 | bytes 37748736 | tf_op jit(solution)/shard_map/dot_general | solution.py:58
  150.9 68.3 %reduce-scatter.2.cloned.1.call-done = bf16[16,4096]{1,0:T(8,128)(2,1)} async-done(((bf16[256,4096]{1,0:T(8,128)(2,1)}), bf16[16,4096]{1,0:T(8,128)(2,1)}) %reduce-scatter.2.cloned.1.call-update) | async-done | bytes 131088 | tf_op jit(solution)/shard_map/reduce_scatter | solution.py:57
  219.2 1.7 add_convert_fusion
  220.9 41.4 %all-gather.2.cloned.1.call-done = bf16[256,4096]{1,0:T(8,128)(2,1)} async-done(((bf16[16,4096]{1,0:T(8,128)(2,1)}), bf16[256,4096]{1,0:T(8,128)(2,1)}) %all-gather.2.cloned.1.call-update) | async-done | bytes 2097168 | tf_op jit(solution)/shard_map/all_gather | solution.py:68
  262.3 15.6 %convolution_convert_fusion = bf16[256,4096]{1,0:T(8,128)(2,1)S(1)} fusion(bf16[256,4096]{1,0:T(8,128)(2,1)} %all-gather.2.cloned.1.call-done, bf16[4096,4096]{1,0:T(8,128)(2,1)} %bitcast.44), kind=kOutput, calls=%fused_computation.23 | convolution fusion | flops 8590983168 | bytes 37748736 | tf_op jit(solution)/shard_map/dot_general | solution.py:67
  278.6 50.4 %all_to_all.43 = bf16[256,16,256]{2,1,0:T(8,128)(2,1)S(1)} all-to-all(bf16[256,16,256]{2,1,0:T(8,128)(2,1)S(1)} %bitcast.47), channel_id=1, replica_groups=mesh['groups'=2,'row'=16] {'row'}, dimensions={0} | all-to-all | bytes 4194304 | tf_op jit(solution)/shard_map/all_to_all | solution.py:73
  329.3 0.8 fusion.6
  330.0 0.8 fusion.7
  330.8 0.8 fusion.8
  331.5 1.6 fusion.12
  (81 shorter events, 5.7 us)
Async XLA Ops:
  7.2 38.2 %copy-start = (bf16[16,256,64]{1,2,0:T(8,128)(2,1)S(1)}, bf16[16,256,64]{1,2,0:T(8,128)(2,1)}, u32[]{:S(2)}) copy-start(bf16[16,256,64]{1,2,0:T(8,128)(2,1)} %param.11) | copy-start | bytes 1572868
  7.2 32.1 %copy-start.2 = (bf16[16,64,64]{2,1,0:T(8,128)(2,1)S(1)}, bf16[16,64,64]{2,1,0:T(8,128)(2,1)}, u32[]{:S(2)}) copy-start(bf16[16,64,64]{2,1,0:T(8,128)(2,1)} %param.12) | copy-start | bytes 393220
  41.2 13.5 %all-to-all-start.1 = ((bf16[16,2,4096]{2,1,0:T(2,128)(2,1)}), bf16[16,2,4096]{2,1,0:T(2,128)(2,1)S(1)}, u32[]{:S(2)}, u32[]{:S(2)}) async-start(bf16[16,2,4096]{2,1,0:T(2,128)(2,1)} %reshape.170), calls=%async_computation.1 | async-start | bytes 524288 | tf_op jit(solution)/shard_map/all_to_all | solution.py:37
  54.7 26.5 %all-to-all-start = ((bf16[32,256,64]{1,2,0:T(8,128)(2,1)}), bf16[32,256,64]{1,2,0:T(8,128)(2,1)S(1)}, u32[]{:S(2)}, u32[]{:S(2)}) async-start(bf16[32,256,64]{1,2,0:T(8,128)(2,1)} %broadcast_select_fusion.4), calls=%async_computation | async-start | bytes 2097152 | tf_op jit(solution)/shard_map/all_to_all | solution.py:36
  71.1 10.7 %copy-start.4 = (bf16[256,64]{0,1:T(8,128)(2,1)S(1)}, bf16[256,64]{0,1:T(8,128)(2,1)}, u32[]{:S(2)}) copy-start(bf16[256,64]{0,1:T(8,128)(2,1)} %param.15) | copy-start | bytes 98308
  85.3 47.7 %all-to-all-start.2 = ((bf16[16,256,256]{2,0,1:T(8,128)(2,1)}), bf16[16,256,256]{2,0,1:T(8,128)(2,1)S(1)}, u32[]{:S(2)}, u32[]{:S(2)}) async-start(bf16[16,256,256]{2,0,1:T(8,128)(2,1)} %copy.16), calls=%async_computation.2 | async-start | bytes 4194304 | tf_op jit(solution)/shard_map/all_to_all | solution.py:51
  92.0 127.2 %reduce-scatter.2.cloned.1.call-start = ((), (), s32[]{:S(2)}) async-start(), calls=%async_computation.5 | async-start | bytes 2228224 | tf_op jit(solution)/shard_map/reduce_scatter | solution.py:57
  150.6 68.6 %copy-start.3 = (f32[16,4096]{1,0:T(8,128)S(1)}, f32[16,4096]{1,0:T(8,128)}, u32[]{:S(2)}) copy-start(f32[16,4096]{1,0:T(8,128)} %param.17) | copy-start | bytes 786436
  150.7 111.7 %all-gather.2.cloned.1.call-start = ((), (), s32[]{:S(2)}) async-start(), calls=%async_computation.6 | async-start | bytes 2228224 | tf_op jit(solution)/shard_map/all_gather | solution.py:68
  330.8 2.3 copy-start.1
Sparse Core Ops, SparseCore 0:
  150.8 68.3 reduce-scatter.1
  221.9 40.3 all-gather.1
where the time goes:
time: 341 us; the launch traced here: 340 us
  waiting for transfers between devices  143 us (42%)
  blocking collectives  64.1 us (19%)
  local copies, waits for them, and re-layouts  46.7 us (14%)
  matrix products  36.2 us (11%)
  other arithmetic  18.6 us (5%)
  between operations  16.3 us (5%)
  starting transfers between devices  14.2 us (4%)
    reduce_scatter x1, waiting for transfers between devices, local(): lax.psum_scatter(lax.dot_general(density_flat, chol_flat, (((1,), (1,)),...  68.3 us
    all_to_all x1, blocking collectives, local(): lax.all_to_all(propagator_part, 'row', split_axis=0, concat_axis=1, tiled...  50.4 us
    all_gather x1, waiting for transfers between devices, local(): lax.all_gather(fields, 'row', axis=0, tiled=True)  41.4 us
    unnamed x18, local copies, waits for them, and re-layouts  27.8 us
    all_to_all x1, waiting for transfers between devices, local(): lax.all_to_all(whole_density, 'row', split_axis=1, concat_axis=0, tiled=T...  18.3 us
    dot_general x1, matrix products, local(): lax.dot_general(density_flat, chol_flat, (((1,), (1,)), ((), ())), prefer...  15.7 us
    dot_general x1, matrix products, local(): jnp.dot(lax.all_gather(fields, 'row', axis=0, tiled=True), chol_flat, pre...  15.6 us
    unnamed x1, blocking collectives  13.8 us
  transfers between devices with their start and end apart: 5, of which 5 were waited for; matrix products, arithmetic and copies ran while one was open for 12% of the time, Pallas kernels for 0%

commit v1 on v0

v1 whole, which is shorter than its diff:
```python
import functools

import jax
import jax.numpy as jnp
from jax import lax
from jax.experimental import pallas as pl
from jax.experimental.pallas import tpu as pltpu
from jax.sharding import PartitionSpec as P

root_step = 0.1
MESH = pl.DeviceIdType.MESH
VM = pltpu.VMEM


def peer(q):
    me = lax.axis_index("row")
    other = me
    bit = 1
    while bit <= q:
        if q & bit:
            other = other + bit - 2 * bit * lax.rem(lax.div(me, bit), 2)
        bit *= 2
    return other


def greet(qs):
    barrier = pltpu.get_barrier_semaphore()
    for q in qs:
        pl.semaphore_signal(barrier, inc=1, device_id={"row": peer(q)}, device_id_type=MESH)
    pl.semaphore_wait(barrier, len(qs))


def density_kernel(pick_ref, theta_ref, trial_ref, out_ref):
    width, electrons = trial_ref.shape
    mine = jnp.dot(pick_ref[...], theta_ref[...], preferred_element_type=jnp.float32).astype(jnp.bfloat16)
    for row in range(theta_ref.shape[1] // electrons):
        out_ref[:, row * width : (row + 1) * width] = lax.dot_general(
            mine[:, row * electrons : (row + 1) * electrons],
            trial_ref[...],
            (((1,), (1,)), ((), ())),
            preferred_element_type=jnp.float32,
        ).astype(jnp.bfloat16)


def stages(bits):
    first = list(range(bits))
    second = [0] + list(range(2, bits)) + [1] if bits > 1 else first
    return first, second


def fields_kernel(n, part_ref, noise_ref, bias_ref, all_ref, got, held, total, send, recv):
    per, cols = noise_ref.shape
    half = cols // 2
    bits = n.bit_length() - 1
    orders = stages(bits)
    greet([1 << b for b in range(bits)])

    def lanes(h):
        return pl.ds(h * half, half)

    def rows(q):
        return pl.ds(q * per, per)

    live = [list(range(n)), list(range(n))]
    flying = [None, None]

    def launch(h, t):
        b = 1 << orders[h][t]
        copies = []
        for q in live[h]:
            if q & b:
                src = part_ref if t == 0 else held
                copy = pltpu.make_async_remote_copy(
                    src_ref=src.at[rows(q), lanes(h)],
                    dst_ref=got.at[rows(q), lanes(h)],
                    send_sem=send.at[h * n + q],
                    recv_sem=recv.at[h * n + q],
                    device_id={"row": peer(b)},
                    device_id_type=MESH,
                )
                copy.start()
                copies.append(copy)
        flying[h] = copies

    for h in range(2):
        launch(h, 0)
    for t in range(bits):
        for h in range(2):
            b = 1 << orders[h][t]
            for copy in flying[h]:
                copy.wait()
            live[h] = [q for q in live[h] if not q & b]
            src = part_ref if t == 0 else held
            for q in live[h]:
                value = src[rows(q), lanes(h)].astype(jnp.float32) + got[rows(q | b), lanes(h)].astype(jnp.float32)
                if t == bits - 1:
                    total[:, lanes(h)] = value
                else:
                    held[rows(q), lanes(h)] = value.astype(jnp.bfloat16)
            if t < bits - 1:
                launch(h, t + 1)

    have = [[0], [0]]

    def spread(h, t):
        b = 1 << orders[h][bits - 1 - t]
        copies = []
        for q in have[h]:
            copy = pltpu.make_async_remote_copy(
                src_ref=all_ref.at[rows(q), lanes(h)],
                dst_ref=all_ref.at[rows(q | b), lanes(h)],
                send_sem=send.at[(2 + h) * n + (q | b)],
                recv_sem=recv.at[(2 + h) * n + (q | b)],
                device_id={"row": peer(b)},
                device_id_type=MESH,
            )
            copy.start()
            copies.append(copy)
        have[h] = have[h] + [q | b for q in have[h]]
        flying[h] = copies

    for h in range(2):
        bias = root_step * total[:, lanes(h)]
        bias_ref[:, lanes(h)] = bias
        all_ref[rows(0), lanes(h)] = (noise_ref[:, lanes(h)] + jnp.clip(bias, -1.0, 1.0)).astype(jnp.bfloat16)
        spread(h, 0)
    for t in range(bits):
        for h in range(2):
            for copy in flying[h]:
                copy.wait()
            if t < bits - 1:
                spread(h, t + 1)


def deal_kernel(n, part_ref, out_ref, own_sem, send, recv):
    me = lax.axis_index("row")
    greet(list(range(1, n)))
    own = pltpu.make_async_copy(part_ref.at[0], out_ref.at[:, me], own_sem)
    own.start()
    copies = []
    for q in range(n - 1, 0, -1):
        copy = pltpu.make_async_remote_copy(
            src_ref=part_ref.at[q],
            dst_ref=out_ref.at[:, me],
            send_sem=send.at[q],
            recv_sem=recv.at[q],
            device_id={"row": peer(q)},
            device_id_type=MESH,
        )
        copy.start()
        copies.append(copy)
    for copy in copies:
        copy.wait()
    own.wait()


def local(walkers, inv_intersection, copies, deal, trial, chol, noise):
    n = lax.axis_size("row")
    me = lax.axis_index("row")
    per, orbitals_n, electrons = walkers.shape
    all_walkers = n * per
    g, own_rows, width = chol.shape
    chol_flat = chol.reshape(g, own_rows * width)

    theta = jnp.einsum("wmk,wkn->wmn", walkers, inv_intersection, preferred_element_type=jnp.float32)
    theta = theta.astype(jnp.bfloat16).reshape(per, n, own_rows * electrons).transpose(1, 0, 2)
    theta_rows = lax.all_to_all(theta, "row", split_axis=0, concat_axis=0, tiled=True)
    theta_rows = theta_rows.reshape(all_walkers, own_rows * electrons)

    everyone = lax.all_to_all(
        jnp.broadcast_to(copies[None], (n, per)), "row", split_axis=0, concat_axis=0, tiled=True
    ).reshape(all_walkers)
    old = jnp.arange(all_walkers, dtype=jnp.int32)
    copy_ends = jnp.sum(jnp.where(old[None, :] <= old[:, None], everyone[None, :], 0), axis=1)
    owners = jnp.arange(n, dtype=jnp.int32)
    residue = jnp.sum(jnp.where(deal[None, :] == owners[:, None], owners[None, :], 0), axis=1)
    slots = jnp.arange(per, dtype=jnp.int32)

    owner = jnp.bitwise_xor(owners, me)
    owner_residue = jnp.sum(jnp.where(deal[None, :] == owner[:, None], owners[None, :], 0), axis=1)
    wanted = (slots[None, :] * n + owner_residue[:, None]).reshape(all_walkers)
    parent = jnp.sum((copy_ends[None, :] <= wanted[:, None]).astype(jnp.int32), axis=1)
    pick = (parent[:, None] == old[None, :]).astype(jnp.bfloat16)

    capacity = (2 * per + n - 1) // n
    ends_by = copy_ends.reshape(n, per)
    starts_dev = ends_by[:, 0] - everyone.reshape(n, per)[:, 0]
    own_first = jnp.sum(jnp.where(owners == me, starts_dev, 0))
    own_count = jnp.sum(copies)
    own_ends = jnp.sum(jnp.where(slots[None, :] <= slots[:, None], copies[None, :], 0), axis=1)
    picks = jnp.arange(capacity, dtype=jnp.int32)[None, :]
    first_hit = own_first + jnp.mod(residue[:, None] - own_first, n)
    positions = (first_hit + picks * n).reshape(-1)
    usable = positions < own_first + own_count
    local_walker = jnp.sum((own_ends[None, :] <= (positions - own_first)[:, None]).astype(jnp.int32), axis=1)
    send_pick = ((local_walker[:, None] == slots[None, :]) & usable[:, None]).astype(jnp.bfloat16)
    flat = walkers.reshape(per, orbitals_n * electrons)
    sent = jnp.dot(send_pick, flat, preferred_element_type=jnp.float32).astype(jnp.bfloat16)
    got = lax.all_to_all(sent, "row", split_axis=0, concat_axis=0, tiled=True)
    own_parent = parent[:per]
    own_wanted = wanted[:per]
    source = own_parent // per
    source_first = jnp.sum(jnp.where(source[:, None] == owners[None, :], starts_dev[None, :], 0), axis=1)
    source_hit = source_first + jnp.mod(owner_residue[0] - source_first, n)
    received = source * capacity + (own_wanted - source_hit) // n
    take = (received[:, None] == jnp.arange(n * capacity)[None, :]).astype(jnp.bfloat16)
    orbitals = jnp.dot(take, got, preferred_element_type=jnp.float32).astype(jnp.bfloat16)
    orbitals = orbitals.reshape(per, orbitals_n, electrons)

    density = pl.pallas_call(
        density_kernel,
        out_shape=jax.ShapeDtypeStruct((all_walkers, own_rows * width), jnp.bfloat16),
        in_specs=[pl.BlockSpec(memory_space=VM)] * 3,
        out_specs=pl.BlockSpec(memory_space=VM),
        name="density",
    )(pick, theta_rows, trial)

    part = lax.dot_general(
        density, chol_flat, (((1,), (1,)), ((), ())), preferred_element_type=jnp.float32
    ).astype(jnp.bfloat16)
    force_bias, fields = pl.pallas_call(
        functools.partial(fields_kernel, n),
        out_shape=(
            jax.ShapeDtypeStruct((per, g), jnp.float32),
            jax.ShapeDtypeStruct((all_walkers, g), jnp.bfloat16),
        ),
        in_specs=[pl.BlockSpec(memory_space=VM)] * 2,
        out_specs=(pl.BlockSpec(memory_space=VM),) * 2,
        scratch_shapes=[
            pltpu.VMEM((all_walkers, g), jnp.bfloat16),
            pltpu.VMEM((all_walkers, g), jnp.bfloat16),
            pltpu.VMEM((per, g), jnp.float32),
            pltpu.SemaphoreType.DMA((4 * n,)),
            pltpu.SemaphoreType.DMA((4 * n,)),
        ],
        compiler_params=pltpu.CompilerParams(collective_id=0, has_side_effects=True),
        name="fields",
    )(part, noise)

    propagator_part = jnp.dot(fields, chol_flat, preferred_element_type=jnp.float32).astype(jnp.bfloat16)
    propagator_part = propagator_part.reshape(n, per, own_rows, width)
    propagator = pl.pallas_call(
        functools.partial(deal_kernel, n),
        out_shape=jax.ShapeDtypeStruct((per, n, own_rows, width), jnp.bfloat16),
        in_specs=[pl.BlockSpec(memory_space=VM)],
        out_specs=pl.BlockSpec(memory_space=VM),
        scratch_shapes=[
            pltpu.SemaphoreType.DMA,
            pltpu.SemaphoreType.DMA((n,)),
            pltpu.SemaphoreType.DMA((n,)),
        ],
        compiler_params=pltpu.CompilerParams(collective_id=1, has_side_effects=True),
        name="deal",
    )(propagator_part)
    propagator = propagator.reshape(per, n * own_rows, width)

    current = orbitals
    summed = orbitals.astype(jnp.float32)
    for degree in range(1, 5):
        product = jnp.einsum("wik,wkn->win", propagator, current, preferred_element_type=jnp.float32)
        current = (root_step / degree * product).astype(jnp.bfloat16)
        summed = summed + current.astype(jnp.float32)
    return (summed.astype(jnp.bfloat16), force_bias)


def solution(mesh):
    in_specs = (
        P(("groups", "row"), None, None),
        P(("groups", "row"), None, None),
        P(("groups", "row")),
        P("groups"),
        P("groups", None),
        P("groups", "row", None),
        P(("groups", "row"), None),
    )
    out_specs = (P(("groups", "row"), None, None), P(("groups", "row"), None))
    return jax.shard_map(local, mesh=mesh, in_specs=in_specs, out_specs=out_specs, check_vma=False)
```

time: 341 us -> 218 us (0.64)
  waiting for transfers between devices: 143 us -> 5.57 us
  Pallas kernels: 0 us -> 109 us
  blocking collectives: 64.1 us -> 0 us
  between operations: 16.3 us -> 2.07 us
  other arithmetic: 18.6 us -> 5.94 us
  local copies, waits for them, and re-layouts: 46.7 us -> 38.4 us
    pallas_call x0 -> x3, Pallas kernels: none -> 109 us  [the longest x1 55 us: local(): pl.pallas_call(functools.partial(deal_kernel, n), out_shape=jax.ShapeDtyp...]
    reduce_scatter x1 -> x0, waiting for transfers between devices: 68.3 us -> none  [local(): lax.psum_scatter(lax.dot_general(density_flat, chol_flat, (((1,), (1,)),...]
    all_to_all x1 -> x0, blocking collectives: 50.4 us -> none  [local(): lax.all_to_all(propagator_part, 'row', split_axis=0, concat_axis=1, tiled...]
    all_gather x1 -> x0, waiting for transfers between devices: 41.4 us -> none  [local(): lax.all_gather(fields, 'row', axis=0, tiled=True)]
    all_to_all x3, waiting for transfers between devices: 33.5 us -> 5.57 us  [the longest x1 5.57 us: local(): lax.all_to_all(theta, 'row', split_axis=0, concat_axis=0, tiled=True)]
    unnamed x1 -> x0, blocking collectives: 13.8 us -> none
    gather x19 -> x0, local copies, waits for them, and re-layouts: 12.6 us -> none  [the longest x9 5.98 us: local(): parent = jnp.searchsorted(copy_ends, wanted, side='right')]
    select_n x19 -> x1, other arithmetic: 8.42 us -> 0.01 us  [local(): source = own_parent // per]
  transfers between devices with their start and end apart: 5 -> 3, of which waited for: 5 -> 1; matrix products, arithmetic and copies ran while one was open for 12% -> 33% of each run, Pallas kernels for 0% -> 50%
where the time goes in v1:
time: 218 us
  Pallas kernels  109 us (50%)
  matrix products  39.5 us (18%)
  local copies, waits for them, and re-layouts  38.4 us (18%)
  starting transfers between devices  17.6 us (8%)
  other arithmetic  5.94 us (3%)
  waiting for transfers between devices  5.57 us (3%)
    pallas_call x1, Pallas kernels, local(): pl.pallas_call(functools.partial(deal_kernel, n), out_shape=jax.ShapeDtyp...  55 us
    pallas_call x1, Pallas kernels, local(): pl.pallas_call(functools.partial(fields_kernel, n), out_shape=(jax.ShapeD...  50.3 us
    unnamed x23, local copies, waits for them, and re-layouts  27.8 us
    dot_general x1, matrix products, local(): lax.dot_general(density, chol_flat, (((1,), (1,)), ((), ())), preferred_e...  16.9 us
    dot_general x1, matrix products, local(): jnp.dot(fields, chol_flat, preferred_element_type=jnp.float32)  15.7 us
    all_to_all x1, starting transfers between devices, local(): lax.all_to_all(jnp.broadcast_to(copies[None], (n, per)), 'row', split_axi...  7.41 us
    all_to_all x1, starting transfers between devices, local(): lax.all_to_all(theta, 'row', split_axis=0, concat_axis=0, tiled=True)  6 us
    all_to_all x1, waiting for transfers between devices, local(): lax.all_to_all(theta, 'row', split_axis=0, concat_axis=0, tiled=True)  5.57 us
  transfers between devices with their start and end apart: 3, of which 1 were waited for; matrix products, arithmetic and copies ran while one was open for 33% of the time, Pallas kernels for 50%

profile of v1, /device:TPU:0, one launch (start us, length us, event | category | flops | bytes accessed | tf_op | source)
XLA Modules:
  0.0 217.8 jit_solution(14233544978080091337)
XLA Ops:
  0.6 0.0 copy-start
  0.6 1.3 broadcast_in_dim.84
  1.9 7.4 %all-to-all-start = ((s32[16,1,16]{2,1,0:T(1,128)}), s32[16,1,16]{2,1,0:T(1,128)S(1)}, u32[]{:S(2)}, u32[]{:S(2)}) async-start(s32[16,1,16]{2,1,0:T(1,128)} %broadcast_in_dim.84), calls=%async_computation | async-start | bytes 16384 | tf_op jit(solution)/shard_map/all_to_all | solution.py:170
  9.4 0.8 select_reduce_fusion.2
  10.2 0.0 copy-done
  10.2 1.4 convolution_convert_fusion.4
  11.6 1.5 copy.34
  13.1 0.0 copy-start.6
  13.1 0.5 copy.37
  13.6 0.7 reshape.137
  14.3 1.1 copy.38
  15.4 0.0 copy-done.6
  15.4 0.7 copy.39.trial_ref
  16.1 22.6 %copy.43 = bf16[512,8,16,256]{3,1,2,0:T(8,128)(2,1)} copy(bf16[512,8,16,256]{3,2,1,0:T(8,128)(2,1)} %bitcast.37) | data formatting | bytes 67108864
  38.7 0.8 reshape.135
  39.5 0.0 copy-done.7
  39.5 0.6 reduce_sum.89
  40.2 0.0 all-to-all-done
  40.2 6.0 %all-to-all-start.2 = ((bf16[16,16,1024]{2,1,0:T(8,128)(2,1)}), bf16[16,16,1024]{2,1,0:T(8,128)(2,1)S(1)}, u32[]{:S(2)}, u32[]{:S(2)}) async-start(bf16[16,16,1024]{2,1,0:T(8,128)(2,1)} %copy.38), calls=%async_computation.2 | async-start | bytes 1048576 | tf_op jit(solution)/shard_map/all_to_all | solution.py:167
  46.2 0.5 broadcast.128
  46.7 0.7 reduce.5
  47.4 0.1 broadcast_in_dim.85
  47.4 0.1 select_reduce_fusion
  47.6 0.1 reshape.134
  47.6 0.1 fusion.10
  47.8 0.6 fusion.16
  48.4 0.0 copy-done.8
  48.4 0.2 select_reduce_fusion.1
  48.6 0.7 fusion.17
  49.2 0.7 add_subtract_fusion
  50.0 0.1 sub.58
  51.3 0.1 add_compare_fusion
  51.3 0.1 lt.29
  51.4 0.1 convert_reduce_fusion.1
  51.5 0.5 convolution_convert_fusion
  52.0 0.1 broadcast_add_fusion
  52.1 0.1 add.96
  52.2 1.5 all_to_all.19
  53.7 0.2 convert_reduce_fusion
  53.9 0.2 select_reduce_fusion.3
  54.0 0.1 fusion.20
  54.1 0.8 fusion.7.pick_ref
  54.9 5.6 %all-to-all-done.2 = bf16[16,16,1024]{2,1,0:T(8,128)(2,1)S(1)} async-done(((bf16[16,16,1024]{2,1,0:T(8,128)(2,1)}), bf16[16,16,1024]{2,1,0:T(8,128)(2,1)S(1)}, u32[]{:S(2)}, u32[]{:S(2)}) %all-to-all-start.2) | async-done | bytes 524320 | tf_op jit(solution)/shard_map/all_to_all | solution.py:167
  60.4 4.2 %all-to-all-start.1 = ((bf16[16,2,16384]{2,1,0:T(2,128)(2,1)}), bf16[16,2,16384]{2,1,0:T(2,128)(2,1)S(1)}, u32[]{:S(2)}, u32[]{:S(2)}) async-start(bf16[16,2,16384]{2,1,0:T(2,128)(2,1)} %all_to_all.19), calls=%async_computation.1 | async-start | bytes 2097152 | tf_op jit(solution)/shard_map/all_to_all | solution.py:199
  64.6 0.0 copy-done.4
  64.6 3.3 %density.1 = bf16[256,4096]{1,0:T(8,128)(2,1)} custom-call(bf16[256,256]{1,0:T(8,128)(2,1)} %fusion.7.pick_ref, bf16[256,1024]{1,0:T(8,128)(2,1)} %bitcast.43, bf16[256,64]{1,0:T(8,128)(2,1)} %copy.39.trial_ref), custom_call_target="tpu_custom_call" | custom-call | tf_op jit(solution)/shard_map/density/pallas_call | solution.py:210
  68.0 16.9 %convolution_convert_fusion.3.part_ref = bf16[256,4096]{1,0:T(8,128)(2,1)} fusion(bf16[256,4096]{1,0:T(8,128)(2,1)} %density.1, bf16[4096,4096]{1,0:T(8,128)(2,1)} %bitcast.38), kind=kOutput, calls=%fused_computation.3 | convolution fusion | flops 8590983168 | bytes 37748736 | tf_op jit(solution)/shard_map/dot_general | solution.py:218
  84.9 50.3 %fields.1 = (f32[16,4096]{1,0:T(8,128)}, bf16[256,4096]{1,0:T(8,128)(2,1)}) custom-call(bf16[256,4096]{1,0:T(8,128)(2,1)} %convolution_convert_fusion.3.part_ref, f32[16,4096]{1,0:T(8,128)} %noise_ref.1), custom_call_target="tpu_custom_call" | custom-call | tf_op jit(solution)/shard_map/fields/pallas_call | solution.py:221
  135.2 15.7 %convolution_convert_fusion.2 = bf16[256,4096]{1,0:T(8,128)(2,1)S(1)} fusion(bf16[256,4096]{1,0:T(8,128)(2,1)} %get-tuple-element.4, bf16[4096,4096]{1,0:T(8,128)(2,1)} %bitcast.39), kind=kOutput, calls=%fused_computation.2 | convolution fusion | flops 8590983168 | bytes 37748736 | tf_op jit(solution)/shard_map/dot_general | solution.py:240
  150.9 1.9 copy.44
  152.9 55.0 %deal.1 = bf16[16,16,16,256]{3,2,1,0:T(8,128)(2,1)} custom-call(bf16[16,16,16,256]{3,2,1,0:T(8,128)(2,1)} %bitcast.40), custom_call_target="tpu_custom_call" | custom-call | tf_op jit(solution)/shard_map/deal/pallas_call | solution.py:242
  207.9 0.0 all-to-all-done.1
  207.9 0.7 all_to_all.21
  208.6 1.1 convolution_convert_fusion.1
  209.8 2.0 reshape.136
  211.8 1.1 copy.35
  212.9 0.8 fusion.6
  213.7 0.8 fusion
  214.5 0.0 copy-start.1
  214.5 0.8 fusion.1
  215.2 0.3 copy-done.3
  215.5 1.6 fusion.5
  217.1 0.0 copy-done.5
  217.1 0.7 copy.46
  (11 shorter events, 0.0 us)
Async XLA Ops:
  0.6 9.5 %copy-start = (bf16[16,64,64]{2,1,0:T(8,128)(2,1)S(1)}, bf16[16,64,64]{2,1,0:T(8,128)(2,1)}, u32[]{:S(2)}) copy-start(bf16[16,64,64]{2,1,0:T(8,128)(2,1)} %param.8) | copy-start | bytes 393220
  1.9 38.2 %all-to-all-start = ((s32[16,1,16]{2,1,0:T(1,128)}), s32[16,1,16]{2,1,0:T(1,128)S(1)}, u32[]{:S(2)}, u32[]{:S(2)}) async-start(s32[16,1,16]{2,1,0:T(1,128)} %broadcast_in_dim.84), calls=%async_computation | async-start | bytes 16384 | tf_op jit(solution)/shard_map/all_to_all | solution.py:170
  13.1 2.3 %copy-start.6 = (bf16[256,64]{0,1:T(8,128)(2,1)S(1)}, bf16[256,64]{0,1:T(8,128)(2,1)}, u32[]{:S(2)}) copy-start(bf16[256,64]{0,1:T(8,128)(2,1)} %param.11) | copy-start | bytes 98308
  16.1 23.4 %copy-start.7 = (s32[16]{0:T(128)S(1)}, s32[16]{0:T(128)}, u32[]{:S(2)}) copy-start(s32[16]{0:T(128)} %param.9) | copy-start | bytes 196
  38.7 9.7 %copy-start.8 = (s32[16]{0:T(128)S(1)}, s32[16]{0:T(128)}, u32[]{:S(2)}) copy-start(s32[16]{0:T(128)} %param.10) | copy-start | bytes 196
  40.2 20.3 %all-to-all-start.2 = ((bf16[16,16,1024]{2,1,0:T(8,128)(2,1)}), bf16[16,16,1024]{2,1,0:T(8,128)(2,1)S(1)}, u32[]{:S(2)}, u32[]{:S(2)}) async-start(bf16[16,16,1024]{2,1,0:T(8,128)(2,1)} %copy.38), calls=%async_computation.2 | async-start | bytes 1048576 | tf_op jit(solution)/shard_map/all_to_all | solution.py:167
  60.4 4.2 %copy-start.4 = (bf16[16,16,1024]{2,1,0:T(8,128)(2,1)}, bf16[16,16,1024]{2,1,0:T(8,128)(2,1)S(1)}, u32[]{:S(2)}) copy-start(bf16[16,16,1024]{2,1,0:T(8,128)(2,1)S(1)} %all-to-all-done.2) | copy-start | bytes 1572868
  60.4 147.5 %all-to-all-start.1 = ((bf16[16,2,16384]{2,1,0:T(2,128)(2,1)}), bf16[16,2,16384]{2,1,0:T(2,128)(2,1)S(1)}, u32[]{:S(2)}, u32[]{:S(2)}) async-start(bf16[16,2,16384]{2,1,0:T(2,128)(2,1)} %all_to_all.19), calls=%async_computation.1 | async-start | bytes 2097152 | tf_op jit(solution)/shard_map/all_to_all | solution.py:199
  208.6 4.3 %copy-start.2 = (bf16[16,16,16,256]{3,2,1,0:T(8,128)(2,1)S(1)}, bf16[16,16,16,256]{3,2,1,0:T(8,128)(2,1)}, u32[]{:S(2)}) copy-start(bf16[16,16,16,256]{3,2,1,0:T(8,128)(2,1)} %deal.1) | copy-start | bytes 6291460
  214.4 1.0 copy-start.3
  214.5 3.3 %copy-start.1 = (bf16[16,64,64]{2,1,0:T(8,128)(2,1)S(1)}, bf16[16,64,64]{2,1,0:T(8,128)(2,1)}, u32[]{:S(2)}) copy-start(bf16[16,64,64]{2,1,0:T(8,128)(2,1)} %param.8) | copy-start | bytes 393220
  215.5 1.6 copy-start.5

commit v2 on v1

--- a/solution.py
+++ b/solution.py
@@ -42,116 +42,152 @@
         ).astype(jnp.bfloat16)
 
 
-def stages(bits):
+def order_of(bits, c):
     first = list(range(bits))
     second = [0] + list(range(2, bits)) + [1] if bits > 1 else first
-    return first, second
-
-
-def fields_kernel(n, part_ref, noise_ref, bias_ref, all_ref, got, held, total, send, recv):
+    return second if c % 2 else first
+
+
+def step_kernel(n, chunks, groups, density_ref, chol_hbm, noise_ref, bias_ref, out_ref,
+                chol_ref, part, got, held, fields, total, product, load, send, recv, own_sem, deal_send, deal_recv):
+    me = lax.axis_index("row")
     per, cols = noise_ref.shape
-    half = cols // 2
+    wide = cols // chunks
+    own_rows, _, width = product.shape
+    tile = min(wide, 256)
     bits = n.bit_length() - 1
-    orders = stages(bits)
-    greet([1 << b for b in range(bits)])
-
-    def lanes(h):
-        return pl.ds(h * half, half)
 
     def rows(q):
         return pl.ds(q * per, per)
 
-    live = [list(range(n)), list(range(n))]
-    flying = [None, None]
-
-    def launch(h, t):
-        b = 1 << orders[h][t]
+    loads = []
+    for c in range(chunks):
+        copy = pltpu.make_async_copy(chol_hbm.at[pl.ds(c * wide, wide)], chol_ref.at[c], load.at[c])
+        copy.start()
+        loads.append(copy)
+    greet(list(range(1, n)))
+
+    live = [list(range(n)) for _ in range(chunks)]
+    have = [[0] for _ in range(chunks)]
+    flying = [None] * chunks
+
+    def move(c, src, dst, pairs, b, base):
         copies = []
-        for q in live[h]:
-            if q & b:
-                src = part_ref if t == 0 else held
-                copy = pltpu.make_async_remote_copy(
-                    src_ref=src.at[rows(q), lanes(h)],
-                    dst_ref=got.at[rows(q), lanes(h)],
-                    send_sem=send.at[h * n + q],
-                    recv_sem=recv.at[h * n + q],
-                    device_id={"row": peer(b)},
-                    device_id_type=MESH,
-                )
-                copy.start()
-                copies.append(copy)
-        flying[h] = copies
-
-    for h in range(2):
-        launch(h, 0)
-    for t in range(bits):
-        for h in range(2):
-            b = 1 << orders[h][t]
-            for copy in flying[h]:
-                copy.wait()
-            live[h] = [q for q in live[h] if not q & b]
-            src = part_ref if t == 0 else held
-            for q in live[h]:
-                value = src[rows(q), lanes(h)].astype(jnp.float32) + got[rows(q | b), lanes(h)].astype(jnp.float32)
-                if t == bits - 1:
-                    total[:, lanes(h)] = value
-                else:
-                    held[rows(q), lanes(h)] = value.astype(jnp.bfloat16)
-            if t < bits - 1:
-                launch(h, t + 1)
-
-    have = [[0], [0]]
-
-    def spread(h, t):
-        b = 1 << orders[h][bits - 1 - t]
-        copies = []
-        for q in have[h]:
+        for q, into in pairs:
             copy = pltpu.make_async_remote_copy(
-                src_ref=all_ref.at[rows(q), lanes(h)],
-                dst_ref=all_ref.at[rows(q | b), lanes(h)],
-                send_sem=send.at[(2 + h) * n + (q | b)],
-                recv_sem=recv.at[(2 + h) * n + (q | b)],
+                src_ref=src.at[c, rows(q)],
+                dst_ref=dst.at[c, rows(into)],
+                send_sem=send.at[base + c * n + into],
+                recv_sem=recv.at[base + c * n + into],
                 device_id={"row": peer(b)},
                 device_id_type=MESH,
             )
             copy.start()
             copies.append(copy)
-        have[h] = have[h] + [q | b for q in have[h]]
-        flying[h] = copies
-
-    for h in range(2):
-        bias = root_step * total[:, lanes(h)]
-        bias_ref[:, lanes(h)] = bias
-        all_ref[rows(0), lanes(h)] = (noise_ref[:, lanes(h)] + jnp.clip(bias, -1.0, 1.0)).astype(jnp.bfloat16)
-        spread(h, 0)
-    for t in range(bits):
-        for h in range(2):
-            for copy in flying[h]:
-                copy.wait()
+        flying[c] = copies
+
+    def scatter(c, t):
+        b = 1 << order_of(bits, c)[t]
+        move(c, part if t == 0 else held, got, [(q, q) for q in live[c] if q & b], b, 0)
+
+    def spread(c, t):
+        b = 1 << order_of(bits, c)[bits - 1 - t]
+        move(c, fields, fields, [(q, q | b) for q in have[c]], b, chunks * n)
+        have[c] = have[c] + [q | b for q in have[c]]
+
+    def land(c):
+        for copy in flying[c]:
+            copy.wait()
+
+    def first_product(c):
+        loads[c].wait()
+
+        def body(i, carry):
+            at = pl.ds(pl.multiple_of(i * tile, tile), tile)
+            part[c, :, at] = lax.dot_general(
+                density_ref[...], chol_ref[c, at, :], (((1,), (1,)), ((), ())), preferred_element_type=jnp.float32
+            ).astype(jnp.bfloat16)
+            return carry
+
+        lax.fori_loop(0, wide // tile, body, 0)
+
+    def second_product(c, low, high):
+        def body(i, carry):
+            at = pl.ds(pl.multiple_of(i * width, width), width)
+            value = jnp.dot(fields[c], chol_ref[c, :, at], preferred_element_type=jnp.float32)
+            if c > 0:
+                value = value + total[i]
+            if c < chunks - 1:
+                total[i] = value
+            else:
+                product[i] = value.astype(jnp.bfloat16)
+            return carry
+
+        lax.fori_loop(low, high, body, 0)
+
+    dealt = []
+
+    def deal(s, low, high):
+        own = pltpu.make_async_copy(
+            product.at[low:high, rows(0)], out_ref.at[pl.ds(me * own_rows + low, high - low)], own_sem.at[s]
+        )
+        own.start()
+        dealt.append(own)
+        for q in range(n - 1, 0, -1):
+            copy = pltpu.make_async_remote_copy(
+                src_ref=product.at[low:high, rows(q)],
+                dst_ref=out_ref.at[pl.ds(me * own_rows + low, high - low)],
+                send_sem=deal_send.at[s * n + q],
+                recv_sem=deal_recv.at[s * n + q],
+                device_id={"row": peer(q)},
+                device_id_type=MESH,
+            )
+            copy.start()
+            dealt.append(copy)
+
+    def stage(c, s):
+        if s == 0:
+            first_product(c)
+            scatter(c, 0)
+        elif s <= bits:
+            t = s - 1
+            b = 1 << order_of(bits, c)[t]
+            land(c)
+            live[c] = [q for q in live[c] if not q & b]
+            src = part if t == 0 else held
+            for q in live[c]:
+                value = src[c, rows(q)].astype(jnp.float32) + got[c, rows(q | b)].astype(jnp.float32)
+                if t < bits - 1:
+                    held[c, rows(q)] = value.astype(jnp.bfloat16)
+                else:
+                    bias = root_step * value
+                    at = pl.ds(c * wide, wide)
+                    bias_ref[:, at] = bias
+                    fields[c, rows(0)] = (noise_ref[:, at] + jnp.clip(bias, -1.0, 1.0)).astype(jnp.bfloat16)
             if t < bits - 1:
-                spread(h, t + 1)
-
-
-def deal_kernel(n, part_ref, out_ref, own_sem, send, recv):
-    me = lax.axis_index("row")
-    greet(list(range(1, n)))
-    own = pltpu.make_async_copy(part_ref.at[0], out_ref.at[:, me], own_sem)
-    own.start()
-    copies = []
-    for q in range(n - 1, 0, -1):
-        copy = pltpu.make_async_remote_copy(
-            src_ref=part_ref.at[q],
-            dst_ref=out_ref.at[:, me],
-            send_sem=send.at[q],
-            recv_sem=recv.at[q],
-            device_id={"row": peer(q)},
-            device_id_type=MESH,
-        )
-        copy.start()
-        copies.append(copy)
-    for copy in copies:
+                scatter(c, t + 1)
+            else:
+                spread(c, 0)
+        else:
+            t = s - bits - 1
+            land(c)
+            if t < bits - 1:
+                spread(c, t + 1)
+
+    last = 2 * bits
+    for tick in range(chunks + last):
+        for c in range(chunks):
+            if 0 <= tick - c <= last:
+                stage(c, tick - c)
+        done = tick - last
+        if 0 <= done < chunks - 1:
+            second_product(done, 0, own_rows)
+    size = own_rows // groups
+    for s in range(groups):
+        second_product(chunks - 1, s * size, (s + 1) * size)
+        deal(s, s * size, (s + 1) * size)
+    for copy in dealt:
         copy.wait()
-    own.wait()
 
 
 def local(walkers, inv_intersection, copies, deal, trial, chol, noise):
@@ -215,44 +251,41 @@
         name="density",
     )(pick, theta_rows, trial)
 
-    part = lax.dot_general(
-        density, chol_flat, (((1,), (1,)), ((), ())), preferred_element_type=jnp.float32
-    ).astype(jnp.bfloat16)
-    force_bias, fields = pl.pallas_call(
-        functools.partial(fields_kernel, n),
+    chunks, groups = 4, 4
+    wide = g // chunks
+    force_bias, dealt = pl.pallas_call(
+        functools.partial(step_kernel, n, chunks, groups),
         out_shape=(
             jax.ShapeDtypeStruct((per, g), jnp.float32),
-            jax.ShapeDtypeStruct((all_walkers, g), jnp.bfloat16),
+            jax.ShapeDtypeStruct((n * own_rows, per, width), jnp.bfloat16),
         ),
-        in_specs=[pl.BlockSpec(memory_space=VM)] * 2,
+        in_specs=[
+            pl.BlockSpec(memory_space=VM),
+            pl.BlockSpec(memory_space=pl.ANY),
+            pl.BlockSpec(memory_space=VM),
+        ],
         out_specs=(pl.BlockSpec(memory_space=VM),) * 2,
         scratch_shapes=[
-            pltpu.VMEM((all_walkers, g), jnp.bfloat16),
-            pltpu.VMEM((all_walkers, g), jnp.bfloat16),
-            pltpu.VMEM((per, g), jnp.float32),
-            pltpu.SemaphoreType.DMA((4 * n,)),
-            pltpu.SemaphoreType.DMA((4 * n,)),
+            pltpu.VMEM((chunks, wide, own_rows * width), jnp.bfloat16),
+            pltpu.VMEM((chunks, all_walkers, wide), jnp.bfloat16),
+            pltpu.VMEM((chunks, all_walkers, wide), jnp.bfloat16),
+            pltpu.VMEM((chunks, all_walkers, wide), jnp.bfloat16),
+            pltpu.VMEM((chunks, all_walkers, wide), jnp.bfloat16),
+            pltpu.VMEM((own_rows, all_walkers, width), jnp.float32),
+            pltpu.VMEM((own_rows, all_walkers, width), jnp.bfloat16),
+            pltpu.SemaphoreType.DMA((chunks,)),
+            pltpu.SemaphoreType.DMA((2 * chunks * n,)),
+            pltpu.SemaphoreType.DMA((2 * chunks * n,)),
+            pltpu.SemaphoreType.DMA((groups,)),
+            pltpu.SemaphoreType.DMA((groups * n,)),
+            pltpu.SemaphoreType.DMA((groups * n,)),
         ],
-        compiler_params=pltpu.CompilerParams(collective_id=0, has_side_effects=True),
-        name="fields",
-    )(part, noise)
-
-    propagator_part = jnp.dot(fields, chol_flat, preferred_element_type=jnp.float32).astype(jnp.bfloat16)
-    propagator_part = propagator_part.reshape(n, per, own_rows, width)
-    propagator = pl.pallas_call(
-        functools.partial(deal_kernel, n),
-        out_shape=jax.ShapeDtypeStruct((per, n, own_rows, width), jnp.bfloat16),
-        in_specs=[pl.BlockSpec(memory_space=VM)],
-        out_specs=pl.BlockSpec(memory_space=VM),
-        scratch_shapes=[
-            pltpu.SemaphoreType.DMA,
-            pltpu.SemaphoreType.DMA((n,)),
-            pltpu.SemaphoreType.DMA((n,)),
-        ],
-        compiler_params=pltpu.CompilerParams(collective_id=1, has_side_effects=True),
-        name="deal",
-    )(propagator_part)
-    propagator = propagator.reshape(per, n * own_rows, width)
+        compiler_params=pltpu.CompilerParams(
+            collective_id=0, has_side_effects=True, vmem_limit_bytes=62 * 2**20
+        ),
+        name="step",
+    )(density, chol_flat, noise)
+    propagator = dealt.transpose(1, 0, 2)
 
     current = orbitals
     summed = orbitals.astype(jnp.float32)

time: 218 us -> 193 us (0.89)
  matrix products: 39.5 us -> 8.22 us
  Pallas kernels: 109 us -> 117 us
  local copies, waits for them, and re-layouts: 38.4 us -> 34.6 us
    dot_general x2 -> x0, matrix products: 32.6 us -> none  [the longest x1 16.9 us: local(): lax.dot_general(density, chol_flat, (((1,), (1,)), ((), ())), preferred_e...]
    pallas_call x2 -> x1, Pallas kernels: 105 us -> 114 us  [local(): pl.pallas_call(functools.partial(step_kernel, n, chunks, groups), out_sha...]
    unnamed x23 -> x20, local copies, waits for them, and re-layouts: 27.8 us -> 25.6 us
  transfers between devices with their start and end apart: 3 -> 3, of which waited for: 1 -> 1; matrix products, arithmetic and copies ran while one was open for 33% -> 19% of each run, Pallas kernels for 50% -> 61%
where the time goes in v2:
time: 193 us
  Pallas kernels  117 us (61%)
  local copies, waits for them, and re-layouts  34.6 us (18%)
  starting transfers between devices  17.6 us (9%)
  matrix products  8.22 us (4%)
  waiting for transfers between devices  6.77 us (4%)
  other arithmetic  6.03 us (3%)
  between operations  2.23 us (1%)
    pallas_call x1, Pallas kernels, local(): pl.pallas_call(functools.partial(step_kernel, n, chunks, groups), out_sha...  114 us
    unnamed x20, local copies, waits for them, and re-layouts  25.6 us
    all_to_all x1, starting transfers between devices, local(): lax.all_to_all(jnp.broadcast_to(copies[None], (n, per)), 'row', split_axi...  7.41 us
    all_to_all x1, waiting for transfers between devices, local(): lax.all_to_all(theta, 'row', split_axis=0, concat_axis=0, tiled=True)  6.77 us
    all_to_all x1, starting transfers between devices, local(): lax.all_to_all(theta, 'row', split_axis=0, concat_axis=0, tiled=True)  6.01 us
    dot_general x4, matrix products, local(): jnp.einsum('wik,wkn->win', propagator, current, preferred_element_type=jn...  6 us
    all_to_all x1, starting transfers between devices, local(): got = lax.all_to_all(sent, 'row', split_axis=0, concat_axis=0, tiled=True)  4.17 us
  transfers between devices with their start and end apart: 3, of which 1 were waited for; matrix products, arithmetic and copies ran while one was open for 19% of the time, Pallas kernels for 61%

profile of v2, /device:TPU:0, one launch (start us, length us, event | category | flops | bytes accessed | tf_op | source)
XLA Modules:
  0.0 192.6 jit_solution(7264162515209291174)
XLA Ops:
  0.6 0.0 copy-start
  0.6 0.0 copy-start.5
  0.7 1.3 broadcast_in_dim.84
  2.0 7.4 %all-to-all-start = ((s32[16,1,16]{2,1,0:T(1,128)}), s32[16,1,16]{2,1,0:T(1,128)S(1)}, u32[]{:S(2)}, u32[]{:S(2)}) async-start(s32[16,1,16]{2,1,0:T(1,128)} %broadcast_in_dim.84), calls=%async_computation | async-start | bytes 16384 | tf_op jit(solution)/shard_map/all_to_all | solution.py:206
  9.4 0.8 select_reduce_fusion.2
  10.2 0.0 copy-done
  10.2 1.4 convolution_convert_fusion.2
  11.6 1.5 copy.50
  13.1 0.0 copy-done.5
  13.1 0.7 reduce_sum.89
  13.8 0.8 reshape.129
  14.7 0.5 copy.53
  15.2 0.0 copy-start.6
  15.2 0.7 reshape.131
  15.9 1.1 copy.54
  17.0 0.0 all-to-all-done
  17.0 6.0 %all-to-all-start.2 = ((bf16[16,16,1024]{2,1,0:T(8,128)(2,1)}), bf16[16,16,1024]{2,1,0:T(8,128)(2,1)S(1)}, u32[]{:S(2)}, u32[]{:S(2)}) async-start(bf16[16,16,1024]{2,1,0:T(8,128)(2,1)} %copy.54), calls=%async_computation.2 | async-start | bytes 1048576 | tf_op jit(solution)/shard_map/all_to_all | solution.py:203
  23.0 0.5 broadcast.128
  23.5 0.7 reduce.5
  24.2 0.1 broadcast_in_dim.85
  24.3 0.1 select_reduce_fusion
  24.4 0.1 reshape.128
  24.5 0.1 fusion.28
  24.6 0.6 fusion.34
  25.2 0.0 copy-done.6
  25.2 0.2 select_reduce_fusion.4
  25.4 0.7 fusion.35
  26.1 0.7 add_subtract_fusion
  26.8 0.1 sub.58
  28.2 0.1 add_compare_fusion
  28.3 0.1 lt.29
  28.4 0.1 convert_reduce_fusion.1
  28.5 0.5 convolution_convert_fusion
  29.0 0.0 copy-start.4
  29.0 1.5 all_to_all.19
  30.5 6.8 %all-to-all-done.2 = bf16[16,16,1024]{2,1,0:T(8,128)(2,1)S(1)} async-done(((bf16[16,16,1024]{2,1,0:T(8,128)(2,1)}), bf16[16,16,1024]{2,1,0:T(8,128)(2,1)S(1)}, u32[]{:S(2)}, u32[]{:S(2)}) %all-to-all-start.2) | async-done | bytes 524320 | tf_op jit(solution)/shard_map/all_to_all | solution.py:203
  37.3 4.2 %all-to-all-start.1 = ((bf16[16,2,16384]{2,1,0:T(2,128)(2,1)}), bf16[16,2,16384]{2,1,0:T(2,128)(2,1)S(1)}, u32[]{:S(2)}, u32[]{:S(2)}) async-start(bf16[16,2,16384]{2,1,0:T(2,128)(2,1)} %all_to_all.19), calls=%async_computation.1 | async-start | bytes 2097152 | tf_op jit(solution)/shard_map/all_to_all | solution.py:235
  41.5 0.0 copy-done.4
  41.5 0.7 copy.55.trial_ref
  42.2 22.6 %copy.63 = bf16[512,8,16,256]{3,1,2,0:T(8,128)(2,1)} copy(bf16[512,8,16,256]{3,2,1,0:T(8,128)(2,1)} %bitcast.23) | data formatting | bytes 67108864
  64.8 0.0 copy-done.2
  64.8 0.1 broadcast_add_fusion
  64.8 0.1 add.96
  64.9 0.2 convert_reduce_fusion
  65.1 0.2 select_reduce_fusion.3
  65.3 0.1 fusion.38
  65.4 0.8 fusion.25.pick_ref
  66.1 3.3 %density.1.density_ref = bf16[256,4096]{1,0:T(8,128)(2,1)} custom-call(bf16[256,256]{1,0:T(8,128)(2,1)} %fusion.25.pick_ref, bf16[256,1024]{1,0:T(8,128)(2,1)} %bitcast.25, bf16[256,64]{1,0:T(8,128)(2,1)} %copy.55.trial_ref), custom_call_target="tpu_custom_call" | custom-call | tf_op jit(solution)/shard_map/density/pallas_call | solution.py:246
  69.4 113.9 %step.1 = (f32[16,4096]{1,0:T(8,128)}, bf16[256,16,256]{2,1,0:T(8,128)(2,1)}) custom-call(bf16[256,4096]{1,0:T(8,128)(2,1)} %density.1.density_ref, bf16[4096,4096]{1,0:T(8,128)(2,1)} %bitcast.22, f32[16,4096]{1,0:T(8,128)} %noise_ref.1), custom_call_target="tpu_custom_call" | custom-call | tf_op jit(solution)/shard_map/step/pallas_call | solution.py:256
  183.3 0.0 all-to-all-done.1
  183.4 0.7 all_to_all.21
  184.0 0.4 convolution_convert_fusion.1
  184.4 1.1 reshape.130
  185.5 0.3 copy.51
  185.8 0.0 copy-start.7
  185.9 2.6 %fusion.22 = bf16[16,256,64]{1,2,0:T(8,128)(2,1)S(1)} fusion(bf16[16,256,64]{2,1,0:T(8,128)(2,1)S(1)} %reshape.130, bf16[16,256,256]{2,0,1:T(8,128)(2,1)} %bitcast.28), kind=kOutput, calls=%fused_computation.17 | convolution fusion | flops 134742016 | bytes 3145728 | tf_op jit(solution)/shard_map/wik,wkn->win/dot_general | solution.py:293
  188.4 0.0 copy-done.7
  188.4 0.8 fusion.4
  189.3 0.0 copy-start.1
  189.3 0.8 fusion.7
  190.1 0.0 copy-start.3
  190.1 1.8 fusion.19
  191.9 0.0 copy-done.3
  191.9 0.7 copy.87
  (5 shorter events, 0.0 us)
Async XLA Ops:
  0.6 9.5 %copy-start = (bf16[16,64,64]{2,1,0:T(8,128)(2,1)S(1)}, bf16[16,64,64]{2,1,0:T(8,128)(2,1)}, u32[]{:S(2)}) copy-start(bf16[16,64,64]{2,1,0:T(8,128)(2,1)} %param.8) | copy-start | bytes 393220
  0.6 12.5 %copy-start.5 = (s32[16]{0:T(128)S(1)}, s32[16]{0:T(128)}, u32[]{:S(2)}) copy-start(s32[16]{0:T(128)} %param.9) | copy-start | bytes 196
  2.0 15.0 %all-to-all-start = ((s32[16,1,16]{2,1,0:T(1,128)}), s32[16,1,16]{2,1,0:T(1,128)S(1)}, u32[]{:S(2)}, u32[]{:S(2)}) async-start(s32[16,1,16]{2,1,0:T(1,128)} %broadcast_in_dim.84), calls=%async_computation | async-start | bytes 16384 | tf_op jit(solution)/shard_map/all_to_all | solution.py:206
  15.2 10.1 %copy-start.6 = (s32[16]{0:T(128)S(1)}, s32[16]{0:T(128)}, u32[]{:S(2)}) copy-start(s32[16]{0:T(128)} %param.10) | copy-start | bytes 196
  17.0 20.3 %all-to-all-start.2 = ((bf16[16,16,1024]{2,1,0:T(8,128)(2,1)}), bf16[16,16,1024]{2,1,0:T(8,128)(2,1)S(1)}, u32[]{:S(2)}, u32[]{:S(2)}) async-start(bf16[16,16,1024]{2,1,0:T(8,128)(2,1)} %copy.54), calls=%async_computation.2 | async-start | bytes 1048576 | tf_op jit(solution)/shard_map/all_to_all | solution.py:203
  29.0 12.5 %copy-start.4 = (bf16[256,64]{0,1:T(8,128)(2,1)S(1)}, bf16[256,64]{0,1:T(8,128)(2,1)}, u32[]{:S(2)}) copy-start(bf16[256,64]{0,1:T(8,128)(2,1)} %param.11) | copy-start | bytes 98308
  37.3 27.5 %copy-start.2 = (bf16[16,16,1024]{2,1,0:T(8,128)(2,1)}, bf16[16,16,1024]{2,1,0:T(8,128)(2,1)S(1)}, u32[]{:S(2)}) copy-start(bf16[16,16,1024]{2,1,0:T(8,128)(2,1)S(1)} %all-to-all-done.2) | copy-start | bytes 1572868
  37.3 146.1 %all-to-all-start.1 = ((bf16[16,2,16384]{2,1,0:T(2,128)(2,1)}), bf16[16,2,16384]{2,1,0:T(2,128)(2,1)S(1)}, u32[]{:S(2)}, u32[]{:S(2)}) async-start(bf16[16,2,16384]{2,1,0:T(2,128)(2,1)} %all_to_all.19), calls=%async_computation.1 | async-start | bytes 2097152 | tf_op jit(solution)/shard_map/all_to_all | solution.py:235
  185.8 2.6 %copy-start.7 = (bf16[256,16,256]{2,1,0:T(8,128)(2,1)S(1)}, bf16[256,16,256]{2,1,0:T(8,128)(2,1)}, u32[]{:S(2)}) copy-start(bf16[256,16,256]{2,1,0:T(8,128)(2,1)} %get-tuple-element.4) | copy-start | bytes 6291460
  189.3 3.3 %copy-start.1 = (bf16[16,64,64]{2,1,0:T(8,128)(2,1)S(1)}, bf16[16,64,64]{2,1,0:T(8,128)(2,1)}, u32[]{:S(2)}) copy-start(bf16[16,64,64]{2,1,0:T(8,128)(2,1)} %param.8) | copy-start | bytes 393220
  190.1 1.8 copy-start.3

commit v3 on v2

--- a/solution.py
+++ b/solution.py
@@ -30,16 +30,64 @@
     pl.semaphore_wait(barrier, len(qs))
 
 
-def density_kernel(pick_ref, theta_ref, trial_ref, out_ref):
+def density_kernel(n, per, capacity, theta_ref, deal_ref, trial_ref, chol_hbm, out_ref, sent_ref, take_ref):
+    me = lax.axis_index("row")
     width, electrons = trial_ref.shape
-    mine = jnp.dot(pick_ref[...], theta_ref[...], preferred_element_type=jnp.float32).astype(jnp.bfloat16)
-    for row in range(theta_ref.shape[1] // electrons):
+    walkers = n * per
+    used = theta_ref.shape[1] - 128
+    own_bits = per.bit_length() - 1
+    cap_bits = capacity.bit_length() - 1
+    slots = n * capacity
+
+    def down(length):
+        return lax.broadcasted_iota(jnp.int32, (length, 1), 0)
+
+    def along(length):
+        return lax.broadcasted_iota(jnp.int32, (1, length), 1)
+
+    count = theta_ref[:, used : used + 1].astype(jnp.float32)
+
+    def counted(mask):
+        return jnp.sum(jnp.where(mask, count, 0.0), axis=0, keepdims=True).astype(jnp.int32)
+
+    deal = deal_ref[...]
+
+    def residue(owner):
+        return jnp.sum(
+            jnp.where(deal == owner, along(n), 0).astype(jnp.float32), axis=1, keepdims=True
+        ).astype(jnp.int32)
+
+    ends = counted(down(walkers) <= along(walkers))
+    starts = counted(down(walkers) < along(walkers))
+
+    def holds(position):
+        return jnp.where((starts <= position) & (position < ends), 1.0, 0.0).astype(jnp.bfloat16)
+
+    new = down(walkers)
+    wanted = jnp.bitwise_and(new, per - 1) * n + residue(jnp.bitwise_xor(jnp.right_shift(new, own_bits), me))
+    mine = jnp.dot(holds(wanted), theta_ref[:, :used], preferred_element_type=jnp.float32).astype(jnp.bfloat16)
+    for row in range(used // electrons):
         out_ref[:, row * width : (row + 1) * width] = lax.dot_general(
             mine[:, row * electrons : (row + 1) * electrons],
             trial_ref[...],
             (((1,), (1,)), ((), ())),
             preferred_element_type=jnp.float32,
         ).astype(jnp.bfloat16)
+
+    line = down(slots)
+    own_first = counted(down(walkers) < me * per)
+    to = residue(jnp.right_shift(line, cap_bits))
+    step = jnp.bitwise_and(line, capacity - 1) * n
+    sent_ref[...] = holds(own_first + jnp.bitwise_and(to - own_first + walkers, n - 1) + step)
+
+    line = along(slots)
+    source = jnp.right_shift(line, cap_bits)
+    first = counted(down(walkers) < source * per)
+    past = counted(down(walkers) < (source + 1) * per)
+    own_residue = residue(jnp.zeros((1, 1), jnp.int32) + me)
+    place = first + jnp.bitwise_and(own_residue - first + walkers, n - 1) + jnp.bitwise_and(line, capacity - 1) * n
+    own_wanted = down(per) * n + own_residue
+    take_ref[...] = jnp.where((place == own_wanted) & (place < past), 1.0, 0.0).astype(jnp.bfloat16)
 
 
 def order_of(bits, c):
@@ -200,56 +248,30 @@
 
     theta = jnp.einsum("wmk,wkn->wmn", walkers, inv_intersection, preferred_element_type=jnp.float32)
     theta = theta.astype(jnp.bfloat16).reshape(per, n, own_rows * electrons).transpose(1, 0, 2)
+    counts = jnp.broadcast_to(copies.astype(jnp.bfloat16)[None, :, None], (n, per, 128))
+    theta = jnp.concatenate([theta, counts], axis=2)
     theta_rows = lax.all_to_all(theta, "row", split_axis=0, concat_axis=0, tiled=True)
-    theta_rows = theta_rows.reshape(all_walkers, own_rows * electrons)
-
-    everyone = lax.all_to_all(
-        jnp.broadcast_to(copies[None], (n, per)), "row", split_axis=0, concat_axis=0, tiled=True
-    ).reshape(all_walkers)
-    old = jnp.arange(all_walkers, dtype=jnp.int32)
-    copy_ends = jnp.sum(jnp.where(old[None, :] <= old[:, None], everyone[None, :], 0), axis=1)
-    owners = jnp.arange(n, dtype=jnp.int32)
-    residue = jnp.sum(jnp.where(deal[None, :] == owners[:, None], owners[None, :], 0), axis=1)
-    slots = jnp.arange(per, dtype=jnp.int32)
-
-    owner = jnp.bitwise_xor(owners, me)
-    owner_residue = jnp.sum(jnp.where(deal[None, :] == owner[:, None], owners[None, :], 0), axis=1)
-    wanted = (slots[None, :] * n + owner_residue[:, None]).reshape(all_walkers)
-    parent = jnp.sum((copy_ends[None, :] <= wanted[:, None]).astype(jnp.int32), axis=1)
-    pick = (parent[:, None] == old[None, :]).astype(jnp.bfloat16)
+    theta_rows = theta_rows.reshape(all_walkers, own_rows * electrons + 128)
 
     capacity = (2 * per + n - 1) // n
-    ends_by = copy_ends.reshape(n, per)
-    starts_dev = ends_by[:, 0] - everyone.reshape(n, per)[:, 0]
-    own_first = jnp.sum(jnp.where(owners == me, starts_dev, 0))
-    own_count = jnp.sum(copies)
-    own_ends = jnp.sum(jnp.where(slots[None, :] <= slots[:, None], copies[None, :], 0), axis=1)
-    picks = jnp.arange(capacity, dtype=jnp.int32)[None, :]
-    first_hit = own_first + jnp.mod(residue[:, None] - own_first, n)
-    positions = (first_hit + picks * n).reshape(-1)
-    usable = positions < own_first + own_count
-    local_walker = jnp.sum((own_ends[None, :] <= (positions - own_first)[:, None]).astype(jnp.int32), axis=1)
-    send_pick = ((local_walker[:, None] == slots[None, :]) & usable[:, None]).astype(jnp.bfloat16)
+    density, sent_all, take = pl.pallas_call(
+        functools.partial(density_kernel, n, per, capacity),
+        out_shape=(
+            jax.ShapeDtypeStruct((all_walkers, own_rows * width), jnp.bfloat16),
+            jax.ShapeDtypeStruct((n * capacity, all_walkers), jnp.bfloat16),
+            jax.ShapeDtypeStruct((per, n * capacity), jnp.bfloat16),
+        ),
+        in_specs=[pl.BlockSpec(memory_space=VM)] * 3 + [pl.BlockSpec(memory_space=pl.ANY)],
+        out_specs=(pl.BlockSpec(memory_space=VM),) * 3,
+        name="density",
+    )(theta_rows, deal.reshape(1, n), trial, chol_flat)
+
     flat = walkers.reshape(per, orbitals_n * electrons)
+    send_pick = lax.dynamic_slice(sent_all, (0, me * per), (n * capacity, per))
     sent = jnp.dot(send_pick, flat, preferred_element_type=jnp.float32).astype(jnp.bfloat16)
     got = lax.all_to_all(sent, "row", split_axis=0, concat_axis=0, tiled=True)
-    own_parent = parent[:per]
-    own_wanted = wanted[:per]
-    source = own_parent // per
-    source_first = jnp.sum(jnp.where(source[:, None] == owners[None, :], starts_dev[None, :], 0), axis=1)
-    source_hit = source_first + jnp.mod(owner_residue[0] - source_first, n)
-    received = source * capacity + (own_wanted - source_hit) // n
-    take = (received[:, None] == jnp.arange(n * capacity)[None, :]).astype(jnp.bfloat16)
     orbitals = jnp.dot(take, got, preferred_element_type=jnp.float32).astype(jnp.bfloat16)
     orbitals = orbitals.reshape(per, orbitals_n, electrons)
-
-    density = pl.pallas_call(
-        density_kernel,
-        out_shape=jax.ShapeDtypeStruct((all_walkers, own_rows * width), jnp.bfloat16),
-        in_specs=[pl.BlockSpec(memory_space=VM)] * 3,
-        out_specs=pl.BlockSpec(memory_space=VM),
-        name="density",
-    )(pick, theta_rows, trial)
 
     chunks, groups = 4, 4
     wide = g // chunks

time: 193 us -> 180 us (0.933)
  waiting for transfers between devices: 6.77 us -> 0.01 us
  Pallas kernels: 117 us -> 123 us
  other arithmetic: 6.03 us -> 0.75 us
  starting transfers between devices: 17.6 us -> 13.4 us
  local copies, waits for them, and re-layouts: 34.6 us -> 32.3 us
    all_to_all x1 -> x0, starting transfers between devices: 7.41 us -> none  [local(): lax.all_to_all(jnp.broadcast_to(copies[None], (n, per)), 'row', split_axi...]
    all_to_all x1, waiting for transfers between devices: 6.77 us -> 0.01 us  [local(): lax.all_to_all(theta, 'row', split_axis=0, concat_axis=0, tiled=True)]
    pallas_call x1, Pallas kernels: 114 us -> 120 us  [local(): pl.pallas_call(functools.partial(step_kernel, n, chunks, groups), out_sha...]
    reduce_sum x8 -> x0, other arithmetic: 2.86 us -> none  [the longest x1 0.77 us: local(): jnp.sum(jnp.where(slots[None, :] <= slots[:, None], copies[None, :], 0),...]
  transfers between devices with their start and end apart: 3 -> 2, of which waited for: 1 -> 0; matrix products, arithmetic and copies ran while one was open for 19% -> 14% of each run, Pallas kernels for 61% -> 67%
where the time goes in v3:
time: 180 us
  Pallas kernels  123 us (68%)
  local copies, waits for them, and re-layouts  32.3 us (18%)
  starting transfers between devices  13.4 us (7%)
  matrix products  8.83 us (5%)
    pallas_call x1, Pallas kernels, local(): pl.pallas_call(functools.partial(step_kernel, n, chunks, groups), out_sha...  120 us
    unnamed x20, local copies, waits for them, and re-layouts  25.8 us
    all_to_all x1, starting transfers between devices, local(): lax.all_to_all(theta, 'row', split_axis=0, concat_axis=0, tiled=True)  7.41 us
    all_to_all x1, starting transfers between devices, local(): got = lax.all_to_all(sent, 'row', split_axis=0, concat_axis=0, tiled=True)  6.02 us
    dot_general x4, matrix products, local(): jnp.einsum('wik,wkn->win', propagator, current, preferred_element_type=jn...  6 us
  transfers between devices with their start and end apart: 2, of which 0 were waited for; matrix products, arithmetic and copies ran while one was open for 14% of the time, Pallas kernels for 67%

profile of v3, /device:TPU:0, one launch (start us, length us, event | category | flops | bytes accessed | tf_op | source)
XLA Modules:
  0.0 179.7 jit_solution(241621323807798044)
XLA Ops:
  0.6 0.0 copy-start
  0.6 0.7 convert_element_type.43
  1.3 0.3 copy-done
  1.6 1.4 convolution_convert_fusion.2
  3.0 0.5 copy.29
  3.5 0.7 reshape.25
  4.2 0.0 copy-start.3
  4.3 0.1 broadcast_in_dim.2
  4.4 0.0 copy-start.5
  4.4 0.9 copy.30
  5.3 7.4 %all-to-all-start = ((bf16[16,16,1152]{2,1,0:T(8,128)(2,1)}), bf16[16,16,1152]{2,1,0:T(8,128)(2,1)S(1)}, u32[]{:S(2)}, u32[]{:S(2)}) async-start(bf16[16,16,1152]{2,1,0:T(8,128)(2,1)} %copy.30), calls=%async_computation | async-start | bytes 1179648 | tf_op jit(solution)/shard_map/all_to_all | solution.py:253
  12.8 0.0 copy-done.3
  12.8 0.5 copy.32
  13.3 0.0 copy-done.5
  13.3 0.7 copy.31.trial_ref
  14.0 0.8 reshape.29
  14.8 22.6 %copy.41 = bf16[512,8,16,256]{3,1,2,0:T(8,128)(2,1)} copy(bf16[512,8,16,256]{3,2,1,0:T(8,128)(2,1)} %bitcast.17) | data formatting | bytes 67108864
  37.4 0.0 all-to-all-done
  37.4 0.0 copy-start.2
  37.4 0.8 copy-done.2
  38.2 3.5 %density.1 = (bf16[256,4096]{1,0:T(8,128)(2,1)}, bf16[32,256]{1,0:T(8,128)(2,1)}, bf16[16,32]{1,0:T(8,128)(2,1)}) custom-call(bf16[256,1152]{1,0:T(8,128)(2,1)} %bitcast.18, s32[1,16]{1,0:T(1,128)} %bitcast.20, bf16[256,64]{1,0:T(8,128)(2,1)} %copy.31.trial_ref, bf16[4096,4096]{1,0:T(8,128)(2,1)} %bitcast.15), custom_call_target="tpu_custom_call" | custom-call | tf_op jit(solution)/shard_map/density/pallas_call | solution.py:257
  41.7 1.2 convolution_convert_fusion
  42.9 1.5 all_to_all.12
  44.4 6.0 %all-to-all-start.1 = ((bf16[16,2,16384]{2,1,0:T(2,128)(2,1)}), bf16[16,2,16384]{2,1,0:T(2,128)(2,1)S(1)}, u32[]{:S(2)}, u32[]{:S(2)}) async-start(bf16[16,2,16384]{2,1,0:T(2,128)(2,1)} %all_to_all.12), calls=%async_computation.1 | async-start | bytes 2097152 | tf_op jit(solution)/shard_map/all_to_all | solution.py:272
  50.4 120.0 %step.1 = (f32[16,4096]{1,0:T(8,128)}, bf16[256,16,256]{2,1,0:T(8,128)(2,1)}) custom-call(bf16[256,4096]{1,0:T(8,128)(2,1)} %get-tuple-element.9.density_ref, bf16[4096,4096]{1,0:T(8,128)(2,1)} %bitcast.16, f32[16,4096]{1,0:T(8,128)} %noise_ref.1), custom_call_target="tpu_custom_call" | custom-call | tf_op jit(solution)/shard_map/step/pallas_call | solution.py:278
  170.5 0.0 copy-start.6
  170.5 0.0 all-to-all-done.1
  170.5 0.4 all_to_all.14
  170.9 0.2 copy-done.6
  171.2 0.3 convolution_convert_fusion.1
  171.4 1.1 reshape.30
  172.6 0.3 copy.33
  172.9 0.0 copy-start.7
  172.9 2.6 %fusion.22 = bf16[16,256,64]{1,2,0:T(8,128)(2,1)S(1)} fusion(bf16[16,256,64]{2,1,0:T(8,128)(2,1)S(1)} %reshape.30, bf16[16,256,256]{2,0,1:T(8,128)(2,1)} %bitcast.21), kind=kOutput, calls=%fused_computation.17 | convolution fusion | flops 134742016 | bytes 3145728 | tf_op jit(solution)/shard_map/wik,wkn->win/dot_general | solution.py:315
  175.5 0.0 copy-done.7
  175.5 0.8 fusion.4
  176.3 0.0 copy-start.1
  176.4 0.8 fusion.7
  177.2 0.0 copy-start.4
  177.2 1.8 fusion.19
  179.0 0.0 copy-done.4
  179.0 0.7 copy.65
  179.7 0.0 copy-done.1
  (1 shorter events, 0.0 us)
Async XLA Ops:
  0.6 1.0 copy-start
  4.2 8.5 %copy-start.3 = (bf16[16,256,64]{1,2,0:T(8,128)(2,1)S(1)}, bf16[16,256,64]{1,2,0:T(8,128)(2,1)}, u32[]{:S(2)}) copy-start(bf16[16,256,64]{1,2,0:T(8,128)(2,1)} %param.7) | copy-start | bytes 1572868
  4.4 8.9 %copy-start.5 = (bf16[256,64]{0,1:T(8,128)(2,1)S(1)}, bf16[256,64]{0,1:T(8,128)(2,1)}, u32[]{:S(2)}) copy-start(bf16[256,64]{0,1:T(8,128)(2,1)} %param.11) | copy-start | bytes 98308
  5.3 32.1 %all-to-all-start = ((bf16[16,16,1152]{2,1,0:T(8,128)(2,1)}), bf16[16,16,1152]{2,1,0:T(8,128)(2,1)S(1)}, u32[]{:S(2)}, u32[]{:S(2)}) async-start(bf16[16,16,1152]{2,1,0:T(8,128)(2,1)} %copy.30), calls=%async_computation | async-start | bytes 1179648 | tf_op jit(solution)/shard_map/all_to_all | solution.py:253
  37.4 0.8 copy-start.2
  44.4 126.1 %all-to-all-start.1 = ((bf16[16,2,16384]{2,1,0:T(2,128)(2,1)}), bf16[16,2,16384]{2,1,0:T(2,128)(2,1)S(1)}, u32[]{:S(2)}, u32[]{:S(2)}) async-start(bf16[16,2,16384]{2,1,0:T(2,128)(2,1)} %all_to_all.12), calls=%async_computation.1 | async-start | bytes 2097152 | tf_op jit(solution)/shard_map/all_to_all | solution.py:272
  170.5 0.7 copy-start.6
  172.9 2.6 %copy-start.7 = (bf16[256,16,256]{2,1,0:T(8,128)(2,1)S(1)}, bf16[256,16,256]{2,1,0:T(8,128)(2,1)}, u32[]{:S(2)}) copy-start(bf16[256,16,256]{2,1,0:T(8,128)(2,1)} %get-tuple-element.10) | copy-start | bytes 6291460
  176.3 3.3 %copy-start.1 = (bf16[16,64,64]{2,1,0:T(8,128)(2,1)S(1)}, bf16[16,64,64]{2,1,0:T(8,128)(2,1)}, u32[]{:S(2)}) copy-start(bf16[16,64,64]{2,1,0:T(8,128)(2,1)} %param.8) | copy-start | bytes 393220
  177.2 1.8 copy-start.4

commit v4 on v3

--- a/solution.py
+++ b/solution.py
@@ -273,7 +273,7 @@
     orbitals = jnp.dot(take, got, preferred_element_type=jnp.float32).astype(jnp.bfloat16)
     orbitals = orbitals.reshape(per, orbitals_n, electrons)
 
-    chunks, groups = 4, 4
+    chunks, groups = 8, 4
     wide = g // chunks
     force_bias, dealt = pl.pallas_call(
         functools.partial(step_kernel, n, chunks, groups),

time: 180 us -> 190 us (1.056)
  Pallas kernels: 123 us -> 133 us
    pallas_call x1, Pallas kernels: 120 us -> 129 us  [local(): pl.pallas_call(functools.partial(step_kernel, n, chunks, groups), out_sha...]
  transfers between devices with their start and end apart: 2 -> 2, of which waited for: 0 -> 0; matrix products, arithmetic and copies ran while one was open for 14% -> 13% of each run, Pallas kernels for 67% -> 68%
where the time goes in v4:
time: 190 us; the launch traced here: 189 us
  Pallas kernels  133 us (70%)
  local copies, waits for them, and re-layouts  32.3 us (17%)
  starting transfers between devices  13.4 us (7%)
  matrix products  8.83 us (5%)
    pallas_call x1, Pallas kernels, local(): pl.pallas_call(functools.partial(step_kernel, n, chunks, groups), out_sha...  129 us
    unnamed x20, local copies, waits for them, and re-layouts  25.6 us
    all_to_all x1, starting transfers between devices, local(): lax.all_to_all(theta, 'row', split_axis=0, concat_axis=0, tiled=True)  7.41 us
    all_to_all x1, starting transfers between devices, local(): got = lax.all_to_all(sent, 'row', split_axis=0, concat_axis=0, tiled=True)  6.02 us
    dot_general x4, matrix products, local(): jnp.einsum('wik,wkn->win', propagator, current, preferred_element_type=jn...  6 us
  transfers between devices with their start and end apart: 2, of which 0 were waited for; matrix products, arithmetic and copies ran while one was open for 13% of the time, Pallas kernels for 68%

profile of v4, /device:TPU:0, one launch (start us, length us, event | category | flops | bytes accessed | tf_op | source)
XLA Modules:
  0.0 189.1 jit_solution(584798847502352914)
XLA Ops:
  0.6 0.0 copy-start
  0.6 0.7 convert_element_type.43
  1.3 0.3 copy-done
  1.6 1.4 convolution_convert_fusion.2
  3.0 0.5 copy.29
  3.5 0.7 reshape.25
  4.2 0.0 copy-start.3
  4.3 0.1 broadcast_in_dim.2
  4.4 0.0 copy-start.5
  4.4 0.9 copy.30
  5.3 7.4 %all-to-all-start = ((bf16[16,16,1152]{2,1,0:T(8,128)(2,1)}), bf16[16,16,1152]{2,1,0:T(8,128)(2,1)S(1)}, u32[]{:S(2)}, u32[]{:S(2)}) async-start(bf16[16,16,1152]{2,1,0:T(8,128)(2,1)} %copy.30), calls=%async_computation | async-start | bytes 1179648 | tf_op jit(solution)/shard_map/all_to_all | solution.py:253
  12.8 0.0 copy-done.3
  12.8 0.5 copy.32
  13.3 0.0 copy-done.5
  13.3 0.7 copy.31.trial_ref
  14.0 0.8 reshape.29
  14.8 22.6 %copy.41 = bf16[512,8,16,256]{3,1,2,0:T(8,128)(2,1)} copy(bf16[512,8,16,256]{3,2,1,0:T(8,128)(2,1)} %bitcast.17) | data formatting | bytes 67108864
  37.4 0.0 all-to-all-done
  37.4 0.0 copy-start.2
  37.4 0.8 copy-done.2
  38.2 3.5 %density.1 = (bf16[256,4096]{1,0:T(8,128)(2,1)}, bf16[32,256]{1,0:T(8,128)(2,1)}, bf16[16,32]{1,0:T(8,128)(2,1)}) custom-call(bf16[256,1152]{1,0:T(8,128)(2,1)} %bitcast.18, s32[1,16]{1,0:T(1,128)} %bitcast.20, bf16[256,64]{1,0:T(8,128)(2,1)} %copy.31.trial_ref, bf16[4096,4096]{1,0:T(8,128)(2,1)} %bitcast.15), custom_call_target="tpu_custom_call" | custom-call | tf_op jit(solution)/shard_map/density/pallas_call | solution.py:257
  41.7 1.2 convolution_convert_fusion
  42.9 1.5 all_to_all.12
  44.4 6.0 %all-to-all-start.1 = ((bf16[16,2,16384]{2,1,0:T(2,128)(2,1)}), bf16[16,2,16384]{2,1,0:T(2,128)(2,1)S(1)}, u32[]{:S(2)}, u32[]{:S(2)}) async-start(bf16[16,2,16384]{2,1,0:T(2,128)(2,1)} %all_to_all.12), calls=%async_computation.1 | async-start | bytes 2097152 | tf_op jit(solution)/shard_map/all_to_all | solution.py:272
  50.4 129.4 %step.1 = (f32[16,4096]{1,0:T(8,128)}, bf16[256,16,256]{2,1,0:T(8,128)(2,1)}) custom-call(bf16[256,4096]{1,0:T(8,128)(2,1)} %get-tuple-element.9.density_ref, bf16[4096,4096]{1,0:T(8,128)(2,1)} %bitcast.16, f32[16,4096]{1,0:T(8,128)} %noise_ref.1), custom_call_target="tpu_custom_call" | custom-call | tf_op jit(solution)/shard_map/step/pallas_call | solution.py:278
  179.9 0.0 copy-start.6
  179.9 0.0 all-to-all-done.1
  179.9 0.7 all_to_all.14
  180.5 0.0 copy-done.6
  180.6 0.3 convolution_convert_fusion.1
  180.8 1.1 reshape.30
  182.0 0.3 copy.33
  182.3 0.0 copy-start.7
  182.3 2.6 %fusion.22 = bf16[16,256,64]{1,2,0:T(8,128)(2,1)S(1)} fusion(bf16[16,256,64]{2,1,0:T(8,128)(2,1)S(1)} %reshape.30, bf16[16,256,256]{2,0,1:T(8,128)(2,1)} %bitcast.21), kind=kOutput, calls=%fused_computation.17 | convolution fusion | flops 134742016 | bytes 3145728 | tf_op jit(solution)/shard_map/wik,wkn->win/dot_general | solution.py:315
  184.9 0.0 copy-done.7
  184.9 0.8 fusion.4
  185.7 0.0 copy-start.1
  185.8 0.8 fusion.7
  186.6 0.0 copy-start.4
  186.6 1.8 fusion.19
  188.4 0.0 copy-done.4
  188.4 0.7 copy.65
  189.1 0.0 copy-done.1
  (1 shorter events, 0.0 us)
Async XLA Ops:
  0.6 1.0 copy-start
  4.2 8.5 %copy-start.3 = (bf16[16,256,64]{1,2,0:T(8,128)(2,1)S(1)}, bf16[16,256,64]{1,2,0:T(8,128)(2,1)}, u32[]{:S(2)}) copy-start(bf16[16,256,64]{1,2,0:T(8,128)(2,1)} %param.7) | copy-start | bytes 1572868
  4.4 8.9 %copy-start.5 = (bf16[256,64]{0,1:T(8,128)(2,1)S(1)}, bf16[256,64]{0,1:T(8,128)(2,1)}, u32[]{:S(2)}) copy-start(bf16[256,64]{0,1:T(8,128)(2,1)} %param.11) | copy-start | bytes 98308
  5.3 32.1 %all-to-all-start = ((bf16[16,16,1152]{2,1,0:T(8,128)(2,1)}), bf16[16,16,1152]{2,1,0:T(8,128)(2,1)S(1)}, u32[]{:S(2)}, u32[]{:S(2)}) async-start(bf16[16,16,1152]{2,1,0:T(8,128)(2,1)} %copy.30), calls=%async_computation | async-start | bytes 1179648 | tf_op jit(solution)/shard_map/all_to_all | solution.py:253
  37.4 0.8 copy-start.2
  44.4 135.5 %all-to-all-start.1 = ((bf16[16,2,16384]{2,1,0:T(2,128)(2,1)}), bf16[16,2,16384]{2,1,0:T(2,128)(2,1)S(1)}, u32[]{:S(2)}, u32[]{:S(2)}) async-start(bf16[16,2,16384]{2,1,0:T(2,128)(2,1)} %all_to_all.12), calls=%async_computation.1 | async-start | bytes 2097152 | tf_op jit(solution)/shard_map/all_to_all | solution.py:272
  179.9 0.7 copy-start.6
  182.3 2.6 %copy-start.7 = (bf16[256,16,256]{2,1,0:T(8,128)(2,1)S(1)}, bf16[256,16,256]{2,1,0:T(8,128)(2,1)}, u32[]{:S(2)}) copy-start(bf16[256,16,256]{2,1,0:T(8,128)(2,1)} %get-tuple-element.10) | copy-start | bytes 6291460
  185.7 3.3 %copy-start.1 = (bf16[16,64,64]{2,1,0:T(8,128)(2,1)S(1)}, bf16[16,64,64]{2,1,0:T(8,128)(2,1)}, u32[]{:S(2)}) copy-start(bf16[16,64,64]{2,1,0:T(8,128)(2,1)} %param.8) | copy-start | bytes 393220
  186.6 1.8 copy-start.4
